TPU v7x, 128 devices: a whole 4x4x4 slice. The times are simulated.
128 devices in a mesh: tile: 32 (over x, z, core), cuts: 4 (over y).
Axes of the slice: x: 4, y: 4, z: 4, core: 2. Of those that a mesh axis runs over, the one named last changes fastest.
Arguments:
- amplitudes: float32 [1024, 128, 128], P(('tile', 'cuts')), may hold values from 0 to 2
- positions: int32 [1024, 2], replicated, may hold values from 0 to 3968, as said below
- probe_field: float32 [2, 128, 128], replicated, may hold values from -4 to 4
- object_slices: float32 [4, 2, 256, 4096], P('cuts', None, None, 'tile'), may hold values from -1 to 1, as said below
Outputs:
- refined_object: float32 [4, 2, 256, 4096], P('cuts', None, None, 'tile')
Inputs may be any that keep to these rules, and one draw needn't show every extreme that they name: `positions`: rows lie in 0 .. 128; every frame's 128 columns lie inside the 4096 columns. A frame's owner tile is its column // 128. Frames are read in blocks of 8 consecutive frames, one block per device of tile+cuts in mesh order; one block holds at most 2 frames of any owner tile, and some block holds exactly 2. For every cuts index, the blocks of that index hold at most 16 frames of any one owner tile, and in every draw some owner tile receives exactly 16 from them. `object_slices`: transmissions have modulus at most 1.
All inputs are finite; a program needn't handle non-finite values.
Results may differ from a plain program's by a relative error of at most 0.015.
Values may be sent and summed in bfloat16 or wider, within the bound.
A program may use at most 128 MiB of HBM per device.

v0:
```python
import math
import jax
import jax.numpy as jnp
from jax import lax
from jax.sharding import PartitionSpec as P

ITERS = 2
STEP_SIZE = 0.05
AMPLITUDE_FLOOR = 0.25


def passed_along(x, axis, by):
    peers = lax.axis_size(axis)
    pairs = [(i, i + by) for i in range(peers) if 0 <= i + by < peers]
    return lax.ppermute(x, axis, pairs)


def block_table(real_part, imag_part):
    upper = jnp.stack([real_part, imag_part], axis=1)
    lower = jnp.stack([-imag_part, real_part], axis=1)
    return jnp.stack([upper, lower], axis=0).astype(jnp.bfloat16)


def make_tables(frame_side):
    highest = lax.Precision.HIGHEST
    index = jnp.arange(frame_side, dtype=jnp.int32)
    product = index[:, None] * index[None, :] % frame_side
    angle = product.astype(jnp.float32) * (2.0 * math.pi / frame_side)
    norm_scale = 1.0 / math.sqrt(frame_side)
    four_real = jnp.cos(angle) * norm_scale
    four_imag = -jnp.sin(angle) * norm_scale
    centred = (index + frame_side // 2) % frame_side - frame_side // 2
    chirp = -math.pi * (centred * centred).astype(jnp.float32) / (4.0 * frame_side)
    chirp_real = jnp.cos(chirp)
    chirp_imag = jnp.sin(chirp)
    left_real = four_real * chirp_real[None, :] + four_imag * chirp_imag[None, :]
    left_imag = four_real * chirp_imag[None, :] - four_imag * chirp_real[None, :]
    prop_real = jnp.dot(left_real, four_real, precision=highest) - jnp.dot(
        left_imag, four_imag, precision=highest
    )
    prop_imag = jnp.dot(left_real, four_imag, precision=highest) + jnp.dot(
        left_imag, four_real, precision=highest
    )
    return (
        block_table(four_real, four_imag),
        block_table(four_real, -four_imag),
        block_table(prop_real, prop_imag),
        block_table(prop_real, -prop_imag),
    )


def right_product(field, table):
    return jnp.einsum(
        "fcij,cjdk->fdik", field.astype(jnp.bfloat16), table, preferred_element_type=jnp.float32
    )


def two_sided(field, table):
    first = right_product(field, table)
    second = right_product(jnp.swapaxes(first, -1, -2), table)
    return jnp.swapaxes(second, -1, -2)


def complex_times(left, right):
    real_part = left[..., 0, :, :] * right[..., 0, :, :] - left[..., 1, :, :] * right[..., 1, :, :]
    imag_part = left[..., 0, :, :] * right[..., 1, :, :] + left[..., 1, :, :] * right[..., 0, :, :]
    return jnp.stack([real_part, imag_part], axis=-3)


def conj_times(left, right):
    real_part = left[..., 0, :, :] * right[..., 0, :, :] + left[..., 1, :, :] * right[..., 1, :, :]
    imag_part = left[..., 0, :, :] * right[..., 1, :, :] - left[..., 1, :, :] * right[..., 0, :, :]
    return jnp.stack([real_part, imag_part], axis=-3)


def frame_patches(windows, probe_field, measured, tables):
    four, four_conj, prop, prop_conj = tables
    slice_count = windows.shape[1]
    wave = complex_times(probe_field[None], windows[:, 0].astype(jnp.float32))
    fields = []
    for level in range(1, slice_count):
        moved = two_sided(wave, prop)
        fields.append(moved)
        wave = complex_times(windows[:, level].astype(jnp.float32), moved)
    far = two_sided(wave, four)
    magnitude = jnp.sqrt(far[:, 0] * far[:, 0] + far[:, 1] * far[:, 1])
    factor = 1.0 - measured / jnp.maximum(magnitude, AMPLITUDE_FLOOR)
    back = two_sided(far * factor[:, None], four_conj)
    patches = [None] * slice_count
    for level in range(slice_count - 1, 0, -1):
        patches[level] = conj_times(fields[level - 1], back)
        back = two_sided(conj_times(windows[:, level].astype(jnp.float32), back), prop_conj)
    patches[0] = conj_times(probe_field[None], back)
    return jnp.stack(patches, axis=1)


def cut_windows(panel, frame_rows, frame_cols, frame_side):
    zero_index = jnp.zeros((), jnp.int32)

    def window_at(row_start, col_start):
        start = (zero_index, zero_index, row_start, col_start)
        return lax.dynamic_slice(
            panel, start, (panel.shape[0], panel.shape[1], frame_side, frame_side)
        )

    return jax.vmap(window_at)(frame_rows, frame_cols)


def place_patches(panel_shape, patches, frame_rows, frame_cols, weights):
    panel_height = panel_shape[-2]
    panel_width = panel_shape[-1]
    frame_side = patches.shape[-1]
    offsets = jnp.arange(frame_side, dtype=jnp.int32)
    col_target = frame_cols[:, None] + offsets[None, :]
    col_onehot = (
        col_target[:, :, None] == jnp.arange(panel_width, dtype=jnp.int32)[None, None, :]
    ).astype(jnp.bfloat16)
    row_target = frame_rows[:, None] + offsets[None, :]
    row_onehot = (
        jnp.arange(panel_height, dtype=jnp.int32)[:, None, None] == row_target[None, :, :]
    ).astype(jnp.bfloat16)
    remain = patches * weights[:, None, None, None, None]
    gathered_sum = jnp.zeros(panel_shape, jnp.float32)
    for piece_index in range(3):
        piece_part = remain.astype(jnp.bfloat16)
        remain = remain - piece_part.astype(jnp.float32)
        placed_cols = jnp.einsum(
            "fscij,fjk->fscik", piece_part, col_onehot, preferred_element_type=jnp.float32
        ).astype(jnp.bfloat16)
        gathered_sum = gathered_sum + jnp.einsum(
            "hfi,fscik->schk", row_onehot, placed_cols, preferred_element_type=jnp.float32
        )
    return gathered_sum


def reduce_gradient(term_part):
    return lax.psum_scatter(term_part, "cuts", scatter_dimension=0, tiled=True)


def add_rim(main_part, moved_rim):
    extra = main_part.shape[-1] - moved_rim.shape[-1]
    return main_part + moved_rim


def body(amplitudes, positions, probe_field, object_slices):
    tile_count = lax.axis_size("tile")
    cut_count = lax.axis_size("cuts")
    tile_id = lax.axis_index("tile")
    cut_id = lax.axis_index("cuts")
    frame_side = probe_field.shape[-1]
    frames_held = amplitudes.shape[0]
    tile_width = object_slices.shape[-1]
    total_frames = positions.shape[0]
    reader_count = total_frames // frames_held
    capacity = max(2, 2 * frames_held // tile_count)
    max_load = 2 * frames_held
    row_list = positions[:, 0]
    col_list = positions[:, 1]
    owner = col_list // tile_width
    owner_grid = owner.reshape(reader_count, frames_held)
    earlier = jnp.tril(jnp.ones((frames_held, frames_held), jnp.int32), -1)
    same_owner = (owner_grid[:, :, None] == owner_grid[:, None, :]).astype(jnp.int32)
    slot_grid = jnp.sum(same_owner * earlier[None], axis=2)
    slot_list = slot_grid.reshape(total_frames)
    reader_self = tile_id * cut_count + cut_id
    my_owner = lax.dynamic_index_in_dim(owner_grid, reader_self, 0, keepdims=False)
    my_slot = lax.dynamic_index_in_dim(slot_grid, reader_self, 0, keepdims=False)
    target = my_owner * capacity + my_slot
    source = (
        jnp.full((tile_count * capacity,), frames_held, jnp.int32)
        .at[target]
        .set(jnp.arange(frames_held, dtype=jnp.int32))
    )
    padded = jnp.concatenate(
        [amplitudes, jnp.zeros((1, frame_side, frame_side), amplitudes.dtype)], axis=0
    )
    outgoing = jnp.take(padded, source, axis=0).reshape(
        tile_count, capacity, frame_side, frame_side
    )
    incoming = lax.all_to_all(outgoing, "tile", split_axis=0, concat_axis=0, tiled=True)
    reader_of = jnp.arange(total_frames, dtype=jnp.int32) // frames_held
    mine = (owner == tile_id) & (reader_of % cut_count == cut_id)
    rank_list = jnp.cumsum(mine.astype(jnp.int32)) - 1
    spot_list = jnp.where(mine, rank_list, max_load)
    chosen = (
        jnp.zeros((max_load,), jnp.int32)
        .at[spot_list]
        .set(jnp.arange(total_frames, dtype=jnp.int32), mode="drop")
    )
    live_weight = jnp.zeros((max_load,), jnp.float32).at[spot_list].set(1.0, mode="drop")
    flat_slot = reader_of // cut_count * capacity + slot_list
    picked = jnp.take(flat_slot, chosen)
    frames_in = jnp.take(
        incoming.reshape(tile_count * capacity, frame_side, frame_side), picked, axis=0
    )
    frame_rows = jnp.take(row_list, chosen)
    frame_cols = jnp.take(col_list, chosen) - tile_id * tile_width
    tables = make_tables(frame_side)
    current = object_slices
    for turn in range(ITERS):
        stacked = lax.all_gather(current.astype(jnp.bfloat16), "cuts", axis=0, tiled=True)
        next_rim = passed_along(stacked, "tile", -1)
        panel = jnp.concatenate([stacked, next_rim], axis=-1)
        windows = cut_windows(panel, frame_rows, frame_cols, frame_side)
        patches = frame_patches(windows, probe_field, frames_in, tables)
        term = place_patches(panel.shape, patches, frame_rows, frame_cols, live_weight)
        moved = passed_along(term[..., tile_width:], "tile", 1)
        share = reduce_gradient(add_rim(term[..., :tile_width], moved))
        current = current - STEP_SIZE * share
    return current


def solution(mesh):
    in_specs = (P(("tile", "cuts"), None, None), P(), P(), P("cuts", None, None, "tile"))
    out_specs = P("cuts", None, None, "tile")
    return jax.shard_map(body, mesh=mesh, in_specs=in_specs, out_specs=out_specs, check_vma=False)
```

profile of v0, /device:TPU:0, one launch (start us, length us, event | category | flops | bytes accessed | tf_op | source)
XLA Modules:
  0.0 458.6 jit_solution(10593045391714817191)
XLA Ops:
  7.5 13.4 %all_gather.6 = bf16[4,2,256,128]{3,2,1,0:T(8,128)(2,1)S(1)} all-gather(bf16[1,2,256,128]{3,2,1,0:T(8,128)(2,1)S(1)} %convert_element_type.304), channel_id=1, replica_groups=mesh['tile'=32,'cuts'=4] {'cuts'}, dimensions={0}, use_global_device_ids=true | all-gather | bytes 655360 | tf_op jit(solution)/shard_map/all_gather | solution.py:201
  29.6 4.5 broadcast_select_fusion
  34.1 9.0 %all-to-all-start = ((f32[32,2,128,128]{3,2,1,0:T(8,128)}), f32[32,2,128,128]{3,2,1,0:T(8,128)}, u32[]{:S(2)}, u32[]{:S(2)}) async-start(f32[32,2,128,128]{3,2,1,0:T(8,128)} %broadcast_select_fusion), calls=%async_computation | async-start | bytes 8388608 | tf_op jit(solution)/shard_map/all_to_all | solution.py:180
  44.9 4.3 scatter_custom_fusion
  52.8 4.8 %scatter_custom_fusion.2 = f32[16]{0:T(128)} fusion(s32[1024]{0:T(1024)S(1)} %bitcast.768, f32[1024]{0:T(1024)S(1)} %broadcast.687, f32[]{:T(128)} %constant.180.clone.1), kind=kCustom, calls=%fused_computation.444 | custom fusion | bytes 68 | tf_op jit(solution)/shard_map/scatter | solution.py:190
  62.3 44.7 %while.2 = (s32[]{:T(128)}, bf16[4,2,256,256]{3,2,1,0:T(8,128)(2,1)S(1)}, s32[16,4]{0,1:T(4,128)S(1)}, bf16[16,4,2,128,128]{4,3,2,0,1:T(8,128)(2,1)}, s32[]{:T(128)}) while((s32[]{:T(128)}, bf16[4,2,256,256]{3,2,1,0:T(8,128)(2,1)S(1)}, s32[16,4]{0,1:T(4,128)S(1)}, bf16[16,4,2,128,128]{4,3,2,0,1:T(8,128)(2,1)}, s32[]{:T(128)}) %tuple.101), condition=%wide.while_cond, body=%wide.while_body.sunk | while | flops 2 | bytes 525937 | solution.py:102
  107.1 5.1 %bitcast_convert_fusion.20 = (f32[16,2,128,128]{3,2,1,0:T(8,128)}, f32[16,2,128,128]{3,2,1,0:T(8,128)}, f32[16,2,128,128]{3,2,1,0:T(8,128)}, f32[16,2,128,128]{3,2,1,0:T(8,128)S(1)}) fusion(bf16[16,4,2,128,128]{4,3,2,0,1:T(8,128)(2,1)} %get-tuple-element.13), kind=kLoop, calls=%fused_computation.200 | loop fusion | flops 2097152 | bytes 12582912 | tf_op jit(solution)/shard_map/convert_element_type | solution.py:92
  133.5 4.1 convolution_bitcast_fusion.14
  137.7 5.4 %add_convert_fusion.9 = (bf16[16,1,128,128]{3,2,1,0:T(8,128)(2,1)}, bf16[16,1,128,128]{3,2,1,0:T(8,128)(2,1)}, f32[16,1,128,128]{3,2,1,0:T(8,128)}, f32[16,1,128,128]{3,2,1,0:T(8,128)}) fusion(f32[16,2,128,128]{3,2,1,0:T(8,128)} %convolution_bitcast_fusion.14, f32[16,2,128,128]{3,2,1,0:T(8,128)} %get-tuple-element.99, ...), kind=kLoop, calls=%fused_computation.251 | loop fusion | flops 3670016 | bytes 9437184 | tf_op jit(solution)/shard_map/convert.26
  143.1 3.3 convolution_bitcast_fusion.8
  146.4 5.4 %add_convert_fusion.8 = (bf16[16,1,128,128]{3,2,1,0:T(8,128)(2,1)}, bf16[16,1,128,128]{3,2,1,0:T(8,128)(2,1)}, f32[16,1,128,128]{3,2,1,0:T(8,128)}, f32[16,1,128,128]{3,2,1,0:T(8,128)}) fusion(f32[16,2,128,128]{3,2,1,0:T(8,128)} %convolution_bitcast_fusion.8, f32[16,2,128,128]{3,2,1,0:T(8,128)} %get-tuple-element.100, ...), kind=kLoop, calls=%fused_computation.249 | loop fusion | flops 3670016 | bytes 9437184 | tf_op jit(solution)/shard_map/convert.24
  155.2 4.7 %add_convert_fusion.7 = (bf16[16,1,128,128]{3,2,1,0:T(8,128)(2,1)}, bf16[16,1,128,128]{3,2,1,0:T(8,128)(2,1)}, f32[16,1,128,128]{3,2,1,0:T(8,128)}, f32[16,1,128,128]{3,2,1,0:T(8,128)}) fusion(f32[16,2,128,128]{3,2,1,0:T(8,128)} %convolution_bitcast_fusion.7, f32[16,2,128,128]{3,2,1,0:T(8,128)} %get-tuple-element.101, ...), kind=kLoop, calls=%fused_computation.247 | loop fusion | flops 3670016 | bytes 9437184 | tf_op jit(solution)/shard_map/convert.22
  167.4 6.4 %fusion.359 = (bf16[16,4,2,128,128]{4,3,2,0,1:T(8,128)(2,1)}, bf16[16,4,2,128,128]{4,3,2,0,1:T(8,128)(2,1)}, bf16[16,4,2,128,128]{4,3,2,0,1:T(8,128)(2,1)}) fusion(f32[16]{0:T(128)S(1)} %copy-done.22, f32[16,1,2,128,128]{4,3,2,0,1:T(8,128)S(1)} %maximum_bitcast_fusion.3, f32[16,1,2,128,128]{4,3,2,0,1:T(8,128)S(1)} %maximum_bitcast_fusion.2, ...), kind=kLoop, calls=%fused_computation.482 | loop fusion | flops 23068672 | bytes 20971584 | tf_op jit(solution)/shard_map/convert_element_type | solution.py:125
  173.8 8.1 %fusion.8 = f32[4,2,256,256,1]{3,2,4,1,0:T(8,128)} fusion(bf16[16,4,2,128,128]{4,3,2,0,1:T(8,128)(2,1)} %get-tuple-element.61, s32[16,128]{1,0:T(8,128)S(1)} %get-tuple-element.150, s32[16,128]{1,0:T(8,128)S(1)} %copy-done.19), kind=kOutput, calls=%fused_computation.25 | convolution fusion | flops 3226468352 | bytes 6307840 | tf_op jit(solution)/shard_map/hfi,fscik->schk/dot_general | solution.py:130
  181.9 8.2 %fusion.6 = f32[4,2,256,256,1]{3,2,4,1,0:T(8,128)} fusion(bf16[16,4,2,128,128]{4,3,2,0,1:T(8,128)(2,1)} %get-tuple-element.62, s32[16,128]{1,0:T(8,128)S(1)} %get-tuple-element.150, s32[16,128]{1,0:T(8,128)S(1)} %copy-done.19), kind=kOutput, calls=%fused_computation.22 | convolution fusion | flops 3226468352 | bytes 6307840 | tf_op jit(solution)/shard_map/hfi,fscik->schk/dot_general | solution.py:130
  190.1 8.3 %fusion.39 = f32[4,2,256,256]{2,3,1,0:T(8,128)S(1)} fusion(f32[4,2,256,256,1]{3,2,4,1,0:T(8,128)} %fusion.6, f32[4,2,256,256,1]{3,2,4,1,0:T(8,128)} %fusion.8, bf16[16,4,2,128,128]{4,3,2,0,1:T(8,128)(2,1)} %get-tuple-element.60, s32[16,128]{1,0:T(8,128)S(1)} %get-tuple-element.150, s32[16,128]{1,0:T(8,128)} %get-tuple-element.151), kind=kOutput, calls=%fused_computation.70 | convolution fusion | flops 3227516928 | bytes 10502144 | tf_op jit(solution)/shard_map/hfi,fscik->schk/dot_general | solution.py:130
  205.3 36.0 %reduce-scatter.3.cloned.1.call-done = f32[1,2,256,128]{2,3,1,0:T(8,128)} async-done(((f32[4,2,256,128]{2,3,1,0:T(8,128)}), f32[1,2,256,128]{2,3,1,0:T(8,128)}) %reduce-scatter.3.cloned.1.call-update) | async-done | bytes 262160 | tf_op jit(solution)/shard_map/reduce_scatter | solution.py:137
  242.4 12.8 %all_gather.7 = bf16[4,2,256,128]{3,2,1,0:T(8,128)(2,1)S(1)} all-gather(bf16[1,2,256,128]{3,2,1,0:T(8,128)(2,1)S(1)} %copy.237), channel_id=1, replica_groups=mesh['tile'=32,'cuts'=4] {'cuts'}, dimensions={0}, use_global_device_ids=true | all-gather | bytes 655360 | tf_op jit(solution)/shard_map/all_gather | solution.py:201
  262.1 46.3 %while.3 = (s32[]{:T(128)}, bf16[4,2,256,256]{3,2,1,0:T(8,128)(2,1)S(1)}, s32[16,4]{0,1:T(4,128)S(1)}, bf16[16,4,2,128,128]{4,3,2,0,1:T(8,128)(2,1)}, s32[]{:T(128)}) while((s32[]{:T(128)}, bf16[4,2,256,256]{3,2,1,0:T(8,128)(2,1)S(1)}, s32[16,4]{0,1:T(4,128)S(1)}, bf16[16,4,2,128,128]{4,3,2,0,1:T(8,128)(2,1)}, s32[]{:T(128)}) %tuple.111), condition=%wide.while_cond.1, body=%wide.while_body.1.sunk | while | flops 2 | bytes 525937 | solution.py:102
  308.4 5.2 %bitcast_convert_fusion.16 = (f32[16,2,128,128]{3,2,1,0:T(8,128)}, f32[16,2,128,128]{3,2,1,0:T(8,128)}, f32[16,2,128,128]{3,2,1,0:T(8,128)}, f32[16,2,128,128]{3,2,1,0:T(8,128)S(1)}) fusion(bf16[16,4,2,128,128]{4,3,2,0,1:T(8,128)(2,1)} %get-tuple-element.21), kind=kLoop, calls=%fused_computation.194 | loop fusion | flops 2097152 | bytes 12582912 | tf_op jit(solution)/shard_map/convert_element_type | solution.py:92
  323.0 3.5 subtract_convert_fusion.6
  329.9 3.6 subtract_convert_fusion.5
  339.9 3.9 convolution_bitcast_fusion.12
  343.8 5.0 %add_convert_fusion.2 = (bf16[16,1,128,128]{3,2,1,0:T(8,128)(2,1)}, bf16[16,1,128,128]{3,2,1,0:T(8,128)(2,1)}, f32[16,1,128,128]{3,2,1,0:T(8,128)S(1)}, f32[16,1,128,128]{3,2,1,0:T(8,128)}) fusion(f32[16,2,128,128]{3,2,1,0:T(8,128)} %convolution_bitcast_fusion.12, f32[16,2,128,128]{3,2,1,0:T(8,128)} %get-tuple-element.77, ...), kind=kLoop, calls=%fused_computation.217 | loop fusion | flops 3670016 | bytes 9437184 | tf_op jit(solution)/shard_map/convert.12
  352.1 5.4 %add_convert_fusion.1 = (bf16[16,1,128,128]{3,2,1,0:T(8,128)(2,1)}, bf16[16,1,128,128]{3,2,1,0:T(8,128)(2,1)}, f32[16,1,128,128]{3,2,1,0:T(8,128)}, f32[16,1,128,128]{3,2,1,0:T(8,128)}) fusion(f32[16,2,128,128]{3,2,1,0:T(8,128)} %convolution_bitcast_fusion.2, f32[16,2,128,128]{3,2,1,0:T(8,128)} %get-tuple-element.78, ...), kind=kLoop, calls=%fused_computation.215 | loop fusion | flops 3670016 | bytes 9437184 | tf_op jit(solution)/shard_map/convert.10
  360.8 4.6 %add_convert_fusion = (bf16[16,1,128,128]{3,2,1,0:T(8,128)(2,1)}, bf16[16,1,128,128]{3,2,1,0:T(8,128)(2,1)}, f32[16,1,128,128]{3,2,1,0:T(8,128)}, f32[16,1,128,128]{3,2,1,0:T(8,128)}) fusion(f32[16,2,128,128]{3,2,1,0:T(8,128)} %convolution_bitcast_fusion.1, f32[16,2,128,128]{3,2,1,0:T(8,128)} %get-tuple-element.79, ...), kind=kLoop, calls=%fused_computation.213 | loop fusion | flops 3670016 | bytes 9437184 | tf_op jit(solution)/shard_map/convert.8
  372.2 6.4 %fusion.358 = (bf16[16,4,2,128,128]{4,3,2,0,1:T(8,128)(2,1)}, bf16[16,4,2,128,128]{4,3,2,0,1:T(8,128)(2,1)}, bf16[16,4,2,128,128]{4,3,2,0,1:T(8,128)(2,1)}) fusion(f32[16]{0:T(128)S(1)} %copy-done.22, f32[16,1,2,128,128]{4,3,2,0,1:T(8,128)S(1)} %maximum_bitcast_fusion.7, f32[16,1,2,128,128]{4,3,2,0,1:T(8,128)S(1)} %maximum_bitcast_fusion.6, ...), kind=kLoop, calls=%fused_computation.481 | loop fusion | flops 23068672 | bytes 20971584 | tf_op jit(solution)/shard_map/convert_element_type | solution.py:125
  378.6 8.1 %fusion.2 = f32[4,2,256,256,1]{3,2,4,1,0:T(8,128)} fusion(bf16[16,4,2,128,128]{4,3,2,0,1:T(8,128)(2,1)} %get-tuple-element.58, s32[16,128]{1,0:T(8,128)S(1)} %get-tuple-element.150, s32[16,128]{1,0:T(8,128)S(1)} %copy-done.20), kind=kOutput, calls=%fused_computation.17 | convolution fusion | flops 3226468352 | bytes 6307840 | tf_op jit(solution)/shard_map/hfi,fscik->schk/dot_general | solution.py:130
  386.8 8.2 %fusion = f32[4,2,256,256,1]{3,2,4,1,0:T(8,128)} fusion(bf16[16,4,2,128,128]{4,3,2,0,1:T(8,128)(2,1)} %get-tuple-element.59, s32[16,128]{1,0:T(8,128)S(1)} %get-tuple-element.150, s32[16,128]{1,0:T(8,128)S(1)} %copy-done.20), kind=kOutput, calls=%fused_computation.14 | convolution fusion | flops 3226468352 | bytes 6307840 | tf_op jit(solution)/shard_map/hfi,fscik->schk/dot_general | solution.py:130
  395.0 8.4 %fusion.38 = f32[4,2,256,256]{2,3,1,0:T(8,128)S(1)} fusion(f32[4,2,256,256,1]{3,2,4,1,0:T(8,128)} %fusion, f32[4,2,256,256,1]{3,2,4,1,0:T(8,128)} %fusion.2, bf16[16,4,2,128,128]{4,3,2,0,1:T(8,128)(2,1)} %get-tuple-element.57, s32[16,128]{1,0:T(8,128)S(1)} %get-tuple-element.150, s32[16,128]{1,0:T(8,128)S(1)} %copy-done.20), kind=kOutput, calls=%fused_computation.65 | convolution fusion | flops 3227516928 | bytes 10502144 | tf_op jit(solution)/shard_map/hfi,fscik->schk/dot_general | solution.py:130
  403.5 8.7 %collective-permute-start.3 = (f32[4,2,256,128]{2,3,1,0:T(8,128)S(1)}, f32[4,2,256,128]{2,3,1,0:T(8,128)S(1)}, u32[]{:S(2)}, u32[]{:S(2)}) collective-permute-start(f32[4,2,256,128]{2,3,1,0:T(8,128)S(1)} %slice.507), channel_id=1, source_target_pairs={{0,4},{4,8},{8,12},{12,16},{16,20},{20,24},{24,28},{28,32},{32,36}... | collective-permute-start | bytes 3145736 | tf_op jit(solution)/shard_map/ppermute | solution.py:15
  415.6 33.9 %reduce-scatter.5.cloned.1.call-done = f32[1,2,256,128]{2,3,1,0:T(8,128)} async-done(((f32[4,2,256,128]{2,3,1,0:T(8,128)}), f32[1,2,256,128]{2,3,1,0:T(8,128)}) %reduce-scatter.5.cloned.1.call-update) | async-done | bytes 262160 | tf_op jit(solution)/shard_map/reduce_scatter | solution.py:137
  (251 shorter events, 195.0 us)
Async XLA Ops:
  20.9 38.2 %collective-permute-start = (bf16[4,2,256,128]{3,2,1,0:T(8,128)(2,1)S(1)}, bf16[4,2,256,128]{3,2,1,0:T(8,128)(2,1)S(1)}, u32[]{:S(2)}, u32[]{:S(2)}) collective-permute-start(bf16[4,2,256,128]{3,2,1,0:T(8,128)(2,1)S(1)} %all_gather.6), channel_id=1, source_target_pairs={{4,0},{8,4},{12,8},{16,12},{20,16},{24,20},{28,24},{32,28},{36,32}... | collective-permute-start | bytes 1572872 | tf_op jit(solution)/shard_map/ppermute | solution.py:15
  34.1 93.5 %all-to-all-start = ((f32[32,2,128,128]{3,2,1,0:T(8,128)}), f32[32,2,128,128]{3,2,1,0:T(8,128)}, u32[]{:S(2)}, u32[]{:S(2)}) async-start(f32[32,2,128,128]{3,2,1,0:T(8,128)} %broadcast_select_fusion), calls=%async_computation | async-start | bytes 8388608 | tf_op jit(solution)/shard_map/all_to_all | solution.py:180
  43.1 198.1 %reduce-scatter.3.cloned.1.call-start = ((), (), s32[]{:S(2)}) async-start(), calls=%async_computation.3 | async-start | bytes 1310720 | tf_op jit(solution)/shard_map/reduce_scatter | solution.py:137
  43.8 15.3 %copy-start.18 = (f32[2,128,128]{2,1,0:T(8,128)S(1)}, f32[2,128,128]{2,1,0:T(8,128)}, u32[]{:S(2)}) copy-start(f32[2,128,128]{2,1,0:T(8,128)} %param.8) | copy-start | bytes 393220
  162.1 1.2 copy-start.9
  162.1 1.5 copy-start.10
  163.6 1.2 copy-start.5
  163.6 1.5 copy-start.6
  165.2 1.2 copy-start.1
  165.2 1.5 copy-start.2
  166.7 0.7 copy-start.22
  167.4 6.4 %copy-start.19 = (s32[16,128]{1,0:T(8,128)S(1)}, s32[16,128]{1,0:T(8,128)}, u32[]{:S(2)}) copy-start(s32[16,128]{1,0:T(8,128)} %get-tuple-element.151) | copy-start | bytes 24580
  198.6 4.4 collective-permute-start.1
  204.1 245.3 %reduce-scatter.5.cloned.1.call-start = ((), (), s32[]{:S(2)}) async-start(), calls=%async_computation.4 | async-start | bytes 1310720 | tf_op jit(solution)/shard_map/reduce_scatter | solution.py:137
  205.3 51.2 %copy-start.11 = (f32[1,2,256,128]{2,3,1,0:T(8,128)}, f32[1,2,256,128]{2,3,1,0:T(8,128)S(1)}, u32[]{:S(2)}) copy-start(f32[1,2,256,128]{2,3,1,0:T(8,128)S(1)} %copy.236) | copy-start | bytes 786436
  255.2 3.8 collective-permute-start.2
  329.9 3.6 copy-start.15
  329.9 3.6 copy-start.16
  333.4 3.3 copy-start.21
  336.8 3.1 copy-start.13
  336.8 3.1 copy-start.14
  367.7 1.2 copy-start.7
  367.7 1.5 copy-start.8
  369.2 1.2 copy-start.3
  369.2 1.5 copy-start.4
  370.8 1.2 copy-start
  372.2 6.4 %copy-start.20 = (s32[16,128]{1,0:T(8,128)S(1)}, s32[16,128]{1,0:T(8,128)}, u32[]{:S(2)}) copy-start(s32[16,128]{1,0:T(8,128)} %get-tuple-element.151) | copy-start | bytes 24580
  403.5 46.0 %copy-start.12 = (f32[1,2,256,128]{2,3,1,0:T(8,128)S(1)}, f32[1,2,256,128]{2,3,1,0:T(8,128)}, u32[]{:S(2)}) copy-start(f32[1,2,256,128]{2,3,1,0:T(8,128)} %copy-done.11) | copy-start | bytes 786436
  403.5 46.0 %copy-start.17 = (f32[1,2,256,128]{2,3,1,0:T(8,128)S(1)}, f32[1,2,256,128]{2,3,1,0:T(8,128)}, u32[]{:S(2)}) copy-start(f32[1,2,256,128]{2,3,1,0:T(8,128)} %reduce-scatter.3.cloned.1.call-done) | copy-start | bytes 786436
  403.5 10.9 %collective-permute-start.3 = (f32[4,2,256,128]{2,3,1,0:T(8,128)S(1)}, f32[4,2,256,128]{2,3,1,0:T(8,128)S(1)}, u32[]{:S(2)}, u32[]{:S(2)}) collective-permute-start(f32[4,2,256,128]{2,3,1,0:T(8,128)S(1)} %slice.507), channel_id=1, source_target_pairs={{0,4},{4,8},{8,12},{12,16},{16,20},{20,24},{24,28},{28,32},{32,36}... | collective-permute-start | bytes 3145736 | tf_op jit(solution)/shard_map/ppermute | solution.py:15
Sparse Core Ops, SparseCore 0:
  204.3 36.9 reduce-scatter.2
  415.7 33.6 reduce-scatter.4
where the time goes:
time: 466 us; the launch traced here: 459 us
  local copies, waits for them, and re-layouts  127 us (27%)
  matrix products  96.5 us (21%)
  other arithmetic  95.2 us (20%)
  waiting for transfers between devices  76.8 us (16%)
  blocking collectives  26.2 us (6%)
  starting transfers between devices  22.6 us (5%)
  between operations  14.4 us (3%)
    gather x96, local copies, waits for them, and re-layouts  90.8 us
    reduce_scatter x2, waiting for transfers between devices, reduce_gradient(): return lax.psum_scatter(term_part, 'cuts', scatter_dimension=0, tiled=True)  69.8 us
    another operation x18, other arithmetic  50.1 us
    dot_general x6, matrix products, place_patches(): jnp.einsum('hfi,fscik->schk', row_onehot, placed_cols, preferred_element_...  49.4 us
    dot_general x16, matrix products, right_product(): jnp.einsum('fcij,cjdk->fdik', field.astype(jnp.bfloat16), table, preferre...  45.2 us
    all_gather x2, blocking collectives, body(): lax.all_gather(current.astype(jnp.bfloat16), 'cuts', axis=0, tiled=True)  26.2 us
    unnamed x49, local copies, waits for them, and re-layouts  15.1 us
    ppermute x4, starting transfers between devices, passed_along(): return lax.ppermute(x, axis, pairs)  13.5 us
  transfers between devices with their start and end apart: 7, of which 5 were waited for; matrix products, arithmetic and copies ran while one was open for 21% of the time, Pallas kernels for 0%

commit v1 on v0

--- a/solution.py
+++ b/solution.py
@@ -7,6 +7,32 @@
 ITERS = 2
 STEP_SIZE = 0.05
 AMPLITUDE_FLOOR = 0.25
+
+
+def get_the_members_all(vec):
+    far_arr, placed, block_next = (lax.axis_size("cuts"), lax.axis_index("cuts"), vec.shape[0])
+    slots = tuple((u * far_arr if dev == 0 else u for dev, u in enumerate(vec.shape)))
+    b_next = lax.dynamic_update_slice_in_dim(
+        jnp.zeros(slots, vec.dtype), vec, placed * block_next, axis=0
+    )
+    even = t1 = vec
+    k0 = 1
+    while k0 < far_arr // 2 + 1:
+        even = lax.ppermute(
+            even, "cuts", tuple(((dev, (dev + 1) % far_arr) for dev in range(far_arr)))
+        )
+        b_next = lax.dynamic_update_slice_in_dim(
+            b_next, even, (placed - k0) % far_arr * block_next, axis=0
+        )
+        if 2 * k0 < far_arr:
+            t1 = lax.ppermute(
+                t1, "cuts", tuple(((dev, (dev - 1) % far_arr) for dev in range(far_arr)))
+            )
+            b_next = lax.dynamic_update_slice_in_dim(
+                b_next, t1, (placed + k0) % far_arr * block_next, axis=0
+            )
+        k0 += 1
+    return b_next
 
 
 def passed_along(x, axis, by):
@@ -198,7 +224,7 @@
     tables = make_tables(frame_side)
     current = object_slices
     for turn in range(ITERS):
-        stacked = lax.all_gather(current.astype(jnp.bfloat16), "cuts", axis=0, tiled=True)
+        stacked = get_the_members_all(current.astype(jnp.bfloat16))
         next_rim = passed_along(stacked, "tile", -1)
         panel = jnp.concatenate([stacked, next_rim], axis=-1)
         windows = cut_windows(panel, frame_rows, frame_cols, frame_side)

time: 466 us -> 488 us (1.047)
  starting transfers between devices: 22.6 us -> 58.7 us
  blocking collectives: 26.2 us -> 0 us
  waiting for transfers between devices: 76.8 us -> 89.2 us
    ppermute x4, starting transfers between devices: 13.5 us -> 43.1 us  [passed_along(): return lax.ppermute(x, axis, pairs)]
    all_gather x2 -> x0, blocking collectives: 26.2 us -> none  [body(): lax.all_gather(current.astype(jnp.bfloat16), 'cuts', axis=0, tiled=True)]
    ppermute x0 -> x6, waiting for transfers between devices: none -> 15 us  [the longest x4 15 us: get_the_members_all(): lax.ppermute(even, 'cuts', tuple(((dev, (dev + 1) % far_arr) for dev in r...]
    ppermute x0 -> x6, starting transfers between devices: none -> 7.11 us  [the longest x2 4.84 us: get_the_members_all(): lax.ppermute(t1, 'cuts', tuple(((dev, (dev - 1) % far_arr) for dev in ran...]
  transfers between devices with their start and end apart: 7 -> 13, of which waited for: 5 -> 9; matrix products, arithmetic and copies ran while one was open for 21% -> 21% of each run, Pallas kernels for 0% -> 0%
where the time goes in v1:
time: 488 us; the launch traced here: 479 us
  local copies, waits for them, and re-layouts  125 us (26%)
  matrix products  96.3 us (20%)
  other arithmetic  95.5 us (20%)
  waiting for transfers between devices  89.2 us (18%)
  starting transfers between devices  58.7 us (12%)
  between operations  14.5 us (3%)
    gather x96, local copies, waits for them, and re-layouts  88.1 us
    reduce_scatter x2, waiting for transfers between devices, reduce_gradient(): return lax.psum_scatter(term_part, 'cuts', scatter_dimension=0, tiled=True)  65.4 us
    another operation x18, other arithmetic  50.3 us
    dot_general x6, matrix products, place_patches(): jnp.einsum('hfi,fscik->schk', row_onehot, placed_cols, preferred_element_...  49.3 us
    dot_general x16, matrix products, right_product(): jnp.einsum('fcij,cjdk->fdik', field.astype(jnp.bfloat16), table, preferre...  45.2 us
    ppermute x4, starting transfers between devices, passed_along(): return lax.ppermute(x, axis, pairs)  43.1 us
    unnamed x49, local copies, waits for them, and re-layouts  15.1 us
    ppermute x4, waiting for transfers between devices, get_the_members_all(): lax.ppermute(even, 'cuts', tuple(((dev, (dev + 1) % far_arr) for dev in r...  15 us
  transfers between devices with their start and end apart: 13, of which 9 were waited for; matrix products, arithmetic and copies ran while one was open for 21% of the time, Pallas kernels for 0%

profile of v1, /device:TPU:0, one launch (start us, length us, event | category | flops | bytes accessed | tf_op | source)
XLA Modules:
  0.0 479.1 jit_solution(5398144170445806705)
XLA Ops:
  18.3 4.5 broadcast_select_fusion
  22.8 8.4 %all-to-all-start = ((f32[32,2,128,128]{3,2,1,0:T(8,128)}), f32[32,2,128,128]{3,2,1,0:T(8,128)}, u32[]{:S(2)}, u32[]{:S(2)}) async-start(f32[32,2,128,128]{3,2,1,0:T(8,128)} %broadcast_select_fusion), calls=%async_computation | async-start | bytes 8388608 | tf_op jit(solution)/shard_map/all_to_all | solution.py:206
  32.6 4.3 scatter_custom_fusion
  41.8 4.8 scatter_custom_fusion.2
  47.0 6.4 %collective-permute-done.2 = bf16[1,2,256,128]{3,2,1,0:T(8,128)(2,1)S(1)} collective-permute-done((bf16[1,2,256,128]{3,2,1,0:T(8,128)(2,1)S(1)}, bf16[1,2,256,128]{3,2,1,0:T(8,128)(2,1)S(1)}, u32[]{:S(2)}, u32[]{:S(2)}) %collective-permute-start.2) | collective-permute-done | bytes 131104 | tf_op jit(solution)/shard_map/ppermute | solution.py:21
  60.4 45.9 %while.2 = (s32[]{:T(128)}, bf16[4,2,256,256]{3,2,1,0:T(8,128)(2,1)S(1)}, s32[16,4]{0,1:T(4,128)S(1)}, bf16[16,4,2,128,128]{4,3,2,0,1:T(8,128)(2,1)}, s32[]{:T(128)}) while((s32[]{:T(128)}, bf16[4,2,256,256]{3,2,1,0:T(8,128)(2,1)S(1)}, s32[16,4]{0,1:T(4,128)S(1)}, bf16[16,4,2,128,128]{4,3,2,0,1:T(8,128)(2,1)}, s32[]{:T(128)}) %tuple.100), condition=%wide.while_cond, body=%wide.while_body.sunk | while | flops 2 | bytes 525937 | solution.py:128
  106.3 5.1 %bitcast_convert_fusion.20 = (f32[16,2,128,128]{3,2,1,0:T(8,128)}, f32[16,2,128,128]{3,2,1,0:T(8,128)}, f32[16,2,128,128]{3,2,1,0:T(8,128)}, f32[16,2,128,128]{3,2,1,0:T(8,128)S(1)}) fusion(bf16[16,4,2,128,128]{4,3,2,0,1:T(8,128)(2,1)} %get-tuple-element.13), kind=kLoop, calls=%fused_computation.200 | loop fusion | flops 2097152 | bytes 12582912 | tf_op jit(solution)/shard_map/convert_element_type | solution.py:118
  132.7 4.1 convolution_bitcast_fusion.14
  136.8 5.5 %add_convert_fusion.9 = (bf16[16,1,128,128]{3,2,1,0:T(8,128)(2,1)}, bf16[16,1,128,128]{3,2,1,0:T(8,128)(2,1)}, f32[16,1,128,128]{3,2,1,0:T(8,128)}, f32[16,1,128,128]{3,2,1,0:T(8,128)}) fusion(f32[16,2,128,128]{3,2,1,0:T(8,128)} %convolution_bitcast_fusion.14, f32[16,2,128,128]{3,2,1,0:T(8,128)} %get-tuple-element.93, ...), kind=kLoop, calls=%fused_computation.251 | loop fusion | flops 3670016 | bytes 9437184 | tf_op jit(solution)/shard_map/convert.26
  145.7 5.5 %add_convert_fusion.8 = (bf16[16,1,128,128]{3,2,1,0:T(8,128)(2,1)}, bf16[16,1,128,128]{3,2,1,0:T(8,128)(2,1)}, f32[16,1,128,128]{3,2,1,0:T(8,128)}, f32[16,1,128,128]{3,2,1,0:T(8,128)}) fusion(f32[16,2,128,128]{3,2,1,0:T(8,128)} %convolution_bitcast_fusion.8, f32[16,2,128,128]{3,2,1,0:T(8,128)} %get-tuple-element.94, ...), kind=kLoop, calls=%fused_computation.249 | loop fusion | flops 3670016 | bytes 9437184 | tf_op jit(solution)/shard_map/convert.24
  154.5 4.7 add_convert_fusion.7
  166.7 6.4 %fusion.359 = (bf16[16,4,2,128,128]{4,3,2,0,1:T(8,128)(2,1)}, bf16[16,4,2,128,128]{4,3,2,0,1:T(8,128)(2,1)}, bf16[16,4,2,128,128]{4,3,2,0,1:T(8,128)(2,1)}) fusion(f32[16]{0:T(128)S(1)} %copy-done.22, f32[16,1,2,128,128]{4,3,2,0,1:T(8,128)S(1)} %maximum_bitcast_fusion.3, f32[16,1,2,128,128]{4,3,2,0,1:T(8,128)S(1)} %maximum_bitcast_fusion.2, ...), kind=kLoop, calls=%fused_computation.490 | loop fusion | flops 23068672 | bytes 20971584 | tf_op jit(solution)/shard_map/convert_element_type | solution.py:151
  173.1 8.1 %fusion.8 = f32[4,2,256,256,1]{3,2,4,1,0:T(8,128)} fusion(bf16[16,4,2,128,128]{4,3,2,0,1:T(8,128)(2,1)} %get-tuple-element.55, s32[16,128]{1,0:T(8,128)S(1)} %get-tuple-element.144, s32[16,128]{1,0:T(8,128)S(1)} %copy-done.19), kind=kOutput, calls=%fused_computation.25 | convolution fusion | flops 3226468352 | bytes 6307840 | tf_op jit(solution)/shard_map/hfi,fscik->schk/dot_general | solution.py:156
  181.2 8.2 %fusion.6 = f32[4,2,256,256,1]{3,2,4,1,0:T(8,128)} fusion(bf16[16,4,2,128,128]{4,3,2,0,1:T(8,128)(2,1)} %get-tuple-element.56, s32[16,128]{1,0:T(8,128)S(1)} %get-tuple-element.144, s32[16,128]{1,0:T(8,128)S(1)} %copy-done.19), kind=kOutput, calls=%fused_computation.22 | convolution fusion | flops 3226468352 | bytes 6307840 | tf_op jit(solution)/shard_map/hfi,fscik->schk/dot_general | solution.py:156
  189.4 8.3 %fusion.39 = f32[4,2,256,256]{2,3,1,0:T(8,128)S(1)} fusion(f32[4,2,256,256,1]{3,2,4,1,0:T(8,128)} %fusion.6, f32[4,2,256,256,1]{3,2,4,1,0:T(8,128)} %fusion.8, bf16[16,4,2,128,128]{4,3,2,0,1:T(8,128)(2,1)} %get-tuple-element.54, s32[16,128]{1,0:T(8,128)S(1)} %get-tuple-element.144, s32[16,128]{1,0:T(8,128)} %get-tuple-element.145), kind=kOutput, calls=%fused_computation.70 | convolution fusion | flops 3227516928 | bytes 10502144 | tf_op jit(solution)/shard_map/hfi,fscik->schk/dot_general | solution.py:156
  197.8 31.7 %collective-permute-start.4 = (f32[4,2,256,128]{2,3,1,0:T(8,128)S(1)}, f32[4,2,256,128]{2,3,1,0:T(8,128)S(1)}, u32[]{:S(2)}, u32[]{:S(2)}) collective-permute-start(f32[4,2,256,128]{2,3,1,0:T(8,128)S(1)} %slice.481), channel_id=1, source_target_pairs={{0,4},{4,8},{8,12},{12,16},{16,20},{20,24},{24,28},{28,32},{32,36}... | collective-permute-start | bytes 3145736 | tf_op jit(solution)/shard_map/ppermute | solution.py:41
  234.1 32.5 %reduce-scatter.3.cloned.1.call-done = f32[1,2,256,128]{2,3,1,0:T(8,128)} async-done(((f32[4,2,256,128]{2,3,1,0:T(8,128)}), f32[1,2,256,128]{2,3,1,0:T(8,128)}) %reduce-scatter.3.cloned.1.call-update) | async-done | bytes 262160 | tf_op jit(solution)/shard_map/reduce_scatter | solution.py:163
  274.2 6.0 %collective-permute-done.7 = bf16[1,2,256,128]{2,3,1,0:T(8,128)(2,1)S(1)} collective-permute-done((bf16[1,2,256,128]{2,3,1,0:T(8,128)(2,1)S(1)}, bf16[1,2,256,128]{2,3,1,0:T(8,128)(2,1)S(1)}, u32[]{:S(2)}, u32[]{:S(2)}) %collective-permute-start.7) | collective-permute-done | bytes 131104 | tf_op jit(solution)/shard_map/ppermute | solution.py:21
  287.3 42.4 %while.3 = (s32[]{:T(128)}, bf16[4,2,256,256]{3,2,1,0:T(8,128)(2,1)S(1)}, s32[16,4]{0,1:T(4,128)S(1)}, bf16[16,4,2,128,128]{4,3,2,0,1:T(8,128)(2,1)}, s32[]{:T(128)}) while((s32[]{:T(128)}, bf16[4,2,256,256]{3,2,1,0:T(8,128)(2,1)S(1)}, s32[16,4]{0,1:T(4,128)S(1)}, bf16[16,4,2,128,128]{4,3,2,0,1:T(8,128)(2,1)}, s32[]{:T(128)}) %tuple.110), condition=%wide.while_cond.1, body=%wide.while_body.1.sunk | while | flops 2 | bytes 525937 | solution.py:128
  329.7 5.2 %bitcast_convert_fusion.16 = (f32[16,2,128,128]{3,2,1,0:T(8,128)}, f32[16,2,128,128]{3,2,1,0:T(8,128)}, f32[16,2,128,128]{3,2,1,0:T(8,128)}, f32[16,2,128,128]{3,2,1,0:T(8,128)S(1)}) fusion(bf16[16,4,2,128,128]{4,3,2,0,1:T(8,128)(2,1)} %get-tuple-element.21), kind=kLoop, calls=%fused_computation.194 | loop fusion | flops 2097152 | bytes 12582912 | tf_op jit(solution)/shard_map/convert_element_type | solution.py:118
  344.4 3.5 subtract_convert_fusion.6
  351.2 3.6 subtract_convert_fusion.5
  361.3 3.9 convolution_bitcast_fusion.12
  365.2 5.0 %add_convert_fusion.2 = (bf16[16,1,128,128]{3,2,1,0:T(8,128)(2,1)}, bf16[16,1,128,128]{3,2,1,0:T(8,128)(2,1)}, f32[16,1,128,128]{3,2,1,0:T(8,128)S(1)}, f32[16,1,128,128]{3,2,1,0:T(8,128)}) fusion(f32[16,2,128,128]{3,2,1,0:T(8,128)} %convolution_bitcast_fusion.12, f32[16,2,128,128]{3,2,1,0:T(8,128)} %get-tuple-element.71, ...), kind=kLoop, calls=%fused_computation.217 | loop fusion | flops 3670016 | bytes 9437184 | tf_op jit(solution)/shard_map/convert.12
  373.5 5.4 %add_convert_fusion.1 = (bf16[16,1,128,128]{3,2,1,0:T(8,128)(2,1)}, bf16[16,1,128,128]{3,2,1,0:T(8,128)(2,1)}, f32[16,1,128,128]{3,2,1,0:T(8,128)}, f32[16,1,128,128]{3,2,1,0:T(8,128)}) fusion(f32[16,2,128,128]{3,2,1,0:T(8,128)} %convolution_bitcast_fusion.2, f32[16,2,128,128]{3,2,1,0:T(8,128)} %get-tuple-element.72, ...), kind=kLoop, calls=%fused_computation.215 | loop fusion | flops 3670016 | bytes 9437184 | tf_op jit(solution)/shard_map/convert.10
  382.2 4.6 add_convert_fusion
  393.6 6.4 %fusion.358 = (bf16[16,4,2,128,128]{4,3,2,0,1:T(8,128)(2,1)}, bf16[16,4,2,128,128]{4,3,2,0,1:T(8,128)(2,1)}, bf16[16,4,2,128,128]{4,3,2,0,1:T(8,128)(2,1)}) fusion(f32[16]{0:T(128)S(1)} %copy-done.22, f32[16,1,2,128,128]{4,3,2,0,1:T(8,128)S(1)} %maximum_bitcast_fusion.7, f32[16,1,2,128,128]{4,3,2,0,1:T(8,128)S(1)} %maximum_bitcast_fusion.6, ...), kind=kLoop, calls=%fused_computation.489 | loop fusion | flops 23068672 | bytes 20971584 | tf_op jit(solution)/shard_map/convert_element_type | solution.py:151
  400.1 8.1 %fusion.2 = f32[4,2,256,256,1]{3,2,4,1,0:T(8,128)} fusion(bf16[16,4,2,128,128]{4,3,2,0,1:T(8,128)(2,1)} %get-tuple-element.52, s32[16,128]{1,0:T(8,128)S(1)} %get-tuple-element.144, s32[16,128]{1,0:T(8,128)S(1)} %copy-done.20), kind=kOutput, calls=%fused_computation.17 | convolution fusion | flops 3226468352 | bytes 6307840 | tf_op jit(solution)/shard_map/hfi,fscik->schk/dot_general | solution.py:156
  408.2 8.2 %fusion = f32[4,2,256,256,1]{3,2,4,1,0:T(8,128)} fusion(bf16[16,4,2,128,128]{4,3,2,0,1:T(8,128)(2,1)} %get-tuple-element.53, s32[16,128]{1,0:T(8,128)S(1)} %get-tuple-element.144, s32[16,128]{1,0:T(8,128)S(1)} %copy-done.20), kind=kOutput, calls=%fused_computation.14 | convolution fusion | flops 3226468352 | bytes 6307840 | tf_op jit(solution)/shard_map/hfi,fscik->schk/dot_general | solution.py:156
  416.3 8.4 %fusion.38 = f32[4,2,256,256]{2,3,1,0:T(8,128)S(1)} fusion(f32[4,2,256,256,1]{3,2,4,1,0:T(8,128)} %fusion, f32[4,2,256,256,1]{3,2,4,1,0:T(8,128)} %fusion.2, bf16[16,4,2,128,128]{4,3,2,0,1:T(8,128)(2,1)} %get-tuple-element.51, s32[16,128]{1,0:T(8,128)S(1)} %get-tuple-element.144, s32[16,128]{1,0:T(8,128)S(1)} %copy-done.20), kind=kOutput, calls=%fused_computation.65 | convolution fusion | flops 3227516928 | bytes 10502144 | tf_op jit(solution)/shard_map/hfi,fscik->schk/dot_general | solution.py:156
  424.8 8.8 %collective-permute-start.9 = (f32[4,2,256,128]{2,3,1,0:T(8,128)S(1)}, f32[4,2,256,128]{2,3,1,0:T(8,128)S(1)}, u32[]{:S(2)}, u32[]{:S(2)}) collective-permute-start(f32[4,2,256,128]{2,3,1,0:T(8,128)S(1)} %slice.507), channel_id=1, source_target_pairs={{0,4},{4,8},{8,12},{12,16},{16,20},{20,24},{24,28},{28,32},{32,36}... | collective-permute-start | bytes 3145736 | tf_op jit(solution)/shard_map/ppermute | solution.py:41
  437.1 32.9 %reduce-scatter.5.cloned.1.call-done = f32[1,2,256,128]{2,3,1,0:T(8,128)} async-done(((f32[4,2,256,128]{2,3,1,0:T(8,128)}), f32[1,2,256,128]{2,3,1,0:T(8,128)}) %reduce-scatter.5.cloned.1.call-update) | async-done | bytes 262160 | tf_op jit(solution)/shard_map/reduce_scatter | solution.py:163
  (273 shorter events, 205.9 us)
Async XLA Ops:
  7.6 38.9 %collective-permute-start = (bf16[1,2,256,128]{3,2,1,0:T(8,128)(2,1)S(1)}, bf16[1,2,256,128]{3,2,1,0:T(8,128)(2,1)S(1)}, u32[]{:S(2)}, u32[]{:S(2)}) collective-permute-start(bf16[1,2,256,128]{3,2,1,0:T(8,128)(2,1)S(1)} %get-tuple-element.46), channel_id=1, source_target_pairs={{0,1},{1,2},{2,3},{3,0},{4,5},{5,6},{6,7},{7,4},{8,9},{9,10},{10,1... | collective-permute-start | bytes 393224 | tf_op jit(solution)/shard_map/ppermute | solution.py:21
  9.4 37.6 %collective-permute-start.1 = (bf16[1,2,256,128]{3,2,1,0:T(8,128)(2,1)S(1)}, bf16[1,2,256,128]{3,2,1,0:T(8,128)(2,1)S(1)}, u32[]{:S(2)}, u32[]{:S(2)}) collective-permute-start(bf16[1,2,256,128]{3,2,1,0:T(8,128)(2,1)S(1)} %get-tuple-element.46), channel_id=1, source_target_pairs={{0,3},{1,0},{2,1},{3,2},{4,7},{5,4},{6,5},{7,6},{8,11},{9,8},{10,9... | collective-permute-start | bytes 393224 | tf_op jit(solution)/shard_map/ppermute | solution.py:28
  22.8 104.1 %all-to-all-start = ((f32[32,2,128,128]{3,2,1,0:T(8,128)}), f32[32,2,128,128]{3,2,1,0:T(8,128)}, u32[]{:S(2)}, u32[]{:S(2)}) async-start(f32[32,2,128,128]{3,2,1,0:T(8,128)} %broadcast_select_fusion), calls=%async_computation | async-start | bytes 8388608 | tf_op jit(solution)/shard_map/all_to_all | solution.py:206
  31.2 235.4 %reduce-scatter.3.cloned.1.call-start = ((), (), s32[]{:S(2)}) async-start(), calls=%async_computation.3 | async-start | bytes 1310720 | tf_op jit(solution)/shard_map/reduce_scatter | solution.py:163
  37.7 17.6 %copy-start.18 = (f32[2,128,128]{2,1,0:T(8,128)S(1)}, f32[2,128,128]{2,1,0:T(8,128)}, u32[]{:S(2)}) copy-start(f32[2,128,128]{2,1,0:T(8,128)} %param.8) | copy-start | bytes 393220
  46.6 6.8 %collective-permute-start.2 = (bf16[1,2,256,128]{3,2,1,0:T(8,128)(2,1)S(1)}, bf16[1,2,256,128]{3,2,1,0:T(8,128)(2,1)S(1)}, u32[]{:S(2)}, u32[]{:S(2)}) collective-permute-start(bf16[1,2,256,128]{3,2,1,0:T(8,128)(2,1)S(1)} %collective-permute-done), channel_id=1, source_target_pairs={{0,1},{1,2},{2,3},{3,0},{4,5},{5,6},{6,7},{7,4},{8,9},{9,10},{10,1... | collective-permute-start | bytes 393224 | tf_op jit(solution)/shard_map/ppermute | solution.py:21
  53.4 3.8 collective-permute-start.3
  161.4 1.2 copy-start.9
  161.4 1.5 copy-start.10
  163.0 1.2 copy-start.5
  163.0 1.5 copy-start.6
  164.5 1.5 copy-start.2
  166.7 6.4 %copy-start.19 = (s32[16,128]{1,0:T(8,128)S(1)}, s32[16,128]{1,0:T(8,128)}, u32[]{:S(2)}) copy-start(s32[16,128]{1,0:T(8,128)} %get-tuple-element.145) | copy-start | bytes 24580
  197.8 33.9 %collective-permute-start.4 = (f32[4,2,256,128]{2,3,1,0:T(8,128)S(1)}, f32[4,2,256,128]{2,3,1,0:T(8,128)S(1)}, u32[]{:S(2)}, u32[]{:S(2)}) collective-permute-start(f32[4,2,256,128]{2,3,1,0:T(8,128)S(1)} %slice.481), channel_id=1, source_target_pairs={{0,4},{4,8},{8,12},{12,16},{16,20},{20,24},{24,28},{28,32},{32,36}... | collective-permute-start | bytes 3145736 | tf_op jit(solution)/shard_map/ppermute | solution.py:41
  233.0 237.1 %reduce-scatter.5.cloned.1.call-start = ((), (), s32[]{:S(2)}) async-start(), calls=%async_computation.4 | async-start | bytes 1310720 | tf_op jit(solution)/shard_map/reduce_scatter | solution.py:163
  234.1 47.6 %copy-start.11 = (f32[1,2,256,128]{2,3,1,0:T(8,128)}, f32[1,2,256,128]{2,3,1,0:T(8,128)S(1)}, u32[]{:S(2)}) copy-start(f32[1,2,256,128]{2,3,1,0:T(8,128)S(1)} %copy.177) | copy-start | bytes 786436
  267.6 6.2 %collective-permute-start.5 = (bf16[1,2,256,128]{2,3,1,0:T(8,128)(2,1)S(1)}, bf16[1,2,256,128]{2,3,1,0:T(8,128)(2,1)S(1)}, u32[]{:S(2)}, u32[]{:S(2)}) collective-permute-start(bf16[1,2,256,128]{2,3,1,0:T(8,128)(2,1)S(1)} %fusion.222), channel_id=1, source_target_pairs={{0,1},{1,2},{2,3},{3,0},{4,5},{5,6},{6,7},{7,4},{8,9},{9,10},{10,1... | collective-permute-start | bytes 393224 | tf_op jit(solution)/shard_map/ppermute | solution.py:21
  267.8 6.3 %collective-permute-start.6 = (bf16[1,2,256,128]{2,3,1,0:T(8,128)(2,1)S(1)}, bf16[1,2,256,128]{2,3,1,0:T(8,128)(2,1)S(1)}, u32[]{:S(2)}, u32[]{:S(2)}) collective-permute-start(bf16[1,2,256,128]{2,3,1,0:T(8,128)(2,1)S(1)} %fusion.222), channel_id=1, source_target_pairs={{0,3},{1,0},{2,1},{3,2},{4,7},{5,4},{6,5},{7,6},{8,11},{9,8},{10,9... | collective-permute-start | bytes 393224 | tf_op jit(solution)/shard_map/ppermute | solution.py:28
  273.9 6.2 %collective-permute-start.7 = (bf16[1,2,256,128]{2,3,1,0:T(8,128)(2,1)S(1)}, bf16[1,2,256,128]{2,3,1,0:T(8,128)(2,1)S(1)}, u32[]{:S(2)}, u32[]{:S(2)}) collective-permute-start(bf16[1,2,256,128]{2,3,1,0:T(8,128)(2,1)S(1)} %collective-permute-done.5), channel_id=1, source_target_pairs={{0,1},{1,2},{2,3},{3,0},{4,5},{5,6},{6,7},{7,4},{8,9},{9,10},{10,1... | collective-permute-start | bytes 393224 | tf_op jit(solution)/shard_map/ppermute | solution.py:21
  280.3 3.8 collective-permute-start.8
  351.2 3.6 copy-start.15
  351.2 3.6 copy-start.16
  354.8 3.4 copy-start.21
  358.2 3.1 copy-start.13
  358.2 3.1 copy-start.14
  389.1 1.2 copy-start.7
  389.1 1.5 copy-start.8
  390.7 1.5 copy-start.4
  393.6 6.4 %copy-start.20 = (s32[16,128]{1,0:T(8,128)S(1)}, s32[16,128]{1,0:T(8,128)}, u32[]{:S(2)}) copy-start(s32[16,128]{1,0:T(8,128)} %get-tuple-element.145) | copy-start | bytes 24580
  424.8 45.2 %copy-start.12 = (f32[1,2,256,128]{2,3,1,0:T(8,128)S(1)}, f32[1,2,256,128]{2,3,1,0:T(8,128)}, u32[]{:S(2)}) copy-start(f32[1,2,256,128]{2,3,1,0:T(8,128)} %copy-done.11) | copy-start | bytes 786436
  424.8 45.2 %copy-start.17 = (f32[1,2,256,128]{2,3,1,0:T(8,128)S(1)}, f32[1,2,256,128]{2,3,1,0:T(8,128)}, u32[]{:S(2)}) copy-start(f32[1,2,256,128]{2,3,1,0:T(8,128)} %reduce-scatter.3.cloned.1.call-done) | copy-start | bytes 786436
  424.8 11.0 %collective-permute-start.9 = (f32[4,2,256,128]{2,3,1,0:T(8,128)S(1)}, f32[4,2,256,128]{2,3,1,0:T(8,128)S(1)}, u32[]{:S(2)}, u32[]{:S(2)}) collective-permute-start(f32[4,2,256,128]{2,3,1,0:T(8,128)S(1)} %slice.507), channel_id=1, source_target_pairs={{0,4},{4,8},{8,12},{12,16},{16,20},{20,24},{24,28},{28,32},{32,36}... | collective-permute-start | bytes 3145736 | tf_op jit(solution)/shard_map/ppermute | solution.py:41
  (4 other events, 4.3 us)
Sparse Core Ops, SparseCore 0:
  233.1 33.4 reduce-scatter.2
  437.2 32.7 reduce-scatter.4
